TPU v7x, 32 devices: a whole 2x2x4 slice. The times are simulated.
32 devices in a mesh: term: 8 (over y, x, core), topic: 4 (over z).
Axes of the slice: x: 2, y: 2, z: 4, core: 2. Of those that a mesh axis runs over, the one named last changes fastest.
Arguments:
- factor: bfloat16 [65536, 512], P('term', 'topic'), may hold values from 1e-06 to 0.05, as said below
- tile_values: bfloat16 [65536, 128], P('term'), may hold values from 0.049804688 to 1
- tile_docs: int32 [8, 128], P('term'), may hold values from 0 to 127, as said below
- codes: float32 [512, 128], P('topic', 'term'), may hold values from 0.1 to 2
- gram_stat: float32 [512, 512], P('topic', 'term'), may hold values from 0 to 4
- data_stat: float32 [65536, 512], P('term', 'topic'), may hold values from 0 to 0.4
Outputs:
- codes_out: float32 [512, 128], P('topic', 'term')
- gram_new: float32 [512, 512], P('topic', 'term')
- data_new: float32 [65536, 512], P('term', 'topic')
Inputs may be any that keep to these rules, and one draw needn't show every extreme that they name: `tile_docs`: each row lists 128 different document numbers. `factor`: positive entries.
All inputs are finite; a program needn't handle non-finite values.
Results may differ from a plain program's by a relative error of at most 0.0003.
Values may be sent and summed in bfloat16 or wider, within the bound.
No kernel may reach another device: no remote copies, remote signals or barrier semaphores. Data moves between devices by JAX's collectives and lax.ppermute only.
A program may use at most 128 MiB of HBM per device.

v0:
```python
import jax
import jax.numpy as jnp
from jax import lax
from jax.sharding import PartitionSpec as P

ITERS = 3
EPSILON = 1e-06
DECAY = 0.5


def contract_rows(left, right):
    return lax.dot_general(
        left, right, (((0,), (0,)), ((), ())), preferred_element_type=jnp.float32
    )


def apply_gram(gram_rows, current):
    return jnp.dot(
        gram_rows,
        lax.all_gather(current, "topic", axis=0, tiled=True),
        precision=lax.Precision.HIGHEST,
        preferred_element_type=jnp.float32,
    )


def per_device(factor, tile_values, tile_docs, codes, gram_stat, data_stat):
    term_count = lax.axis_size("term")
    documents = codes.shape[1] * term_count
    onehot = (tile_docs[0][:, None] == jnp.arange(documents, dtype=jnp.int32)[None, :]).astype(
        jnp.bfloat16
    )
    batch = jnp.dot(tile_values, onehot, preferred_element_type=jnp.float32).astype(jnp.bfloat16)
    partial_data = contract_rows(factor, batch)
    data_share = lax.psum_scatter(partial_data, "term", scatter_dimension=1, tiled=True)
    row_block = lax.all_to_all(factor, "topic", split_axis=0, concat_axis=1, tiled=True)
    gram_part = lax.psum_scatter(
        contract_rows(row_block, row_block), "topic", scatter_dimension=0, tiled=True
    )
    gram_rows = lax.psum(gram_part, "term")
    current = codes
    for update in range(ITERS):
        current = current * data_share / (apply_gram(gram_rows, current) + EPSILON)
    outer = lax.dot_general(
        current,
        lax.all_gather(current, "topic", axis=0, tiled=True),
        (((1,), (1,)), ((), ())),
        precision=lax.Precision.HIGHEST,
        preferred_element_type=jnp.float32,
    )
    outer_share = lax.psum_scatter(outer, "term", scatter_dimension=1, tiled=True)
    gram_new = DECAY * gram_stat + outer_share / documents
    code_row = lax.all_gather(current, "term", axis=1, tiled=True)
    widened = batch.astype(jnp.float32)
    product = lax.dot_general(
        widened,
        code_row,
        (((1,), (1,)), ((), ())),
        precision=lax.Precision.HIGHEST,
        preferred_element_type=jnp.float32,
    )
    data_new = DECAY * data_stat + product / documents
    return (current, gram_new, data_new)


def solution(mesh):
    placed = (
        P("term", "topic"),
        P("term", None),
        P("term", None),
        P("topic", "term"),
        P("topic", "term"),
        P("term", "topic"),
    )
    return jax.shard_map(
        per_device,
        mesh=mesh,
        in_specs=placed,
        out_specs=(P("topic", "term"), P("topic", "term"), P("term", "topic")),
        check_vma=False,
    )
```

profile of v0, /device:TPU:0, one launch (start us, length us, event | category | flops | bytes accessed | tf_op | source)
XLA Modules:
  0.0 284.7 jit_solution(639582228280729309)
XLA Ops:
  7.2 54.8 %all_to_all.19 = bf16[4,2048,128]{2,1,0:T(8,128)(2,1)} all-to-all(bf16[4,2048,128]{2,1,0:T(8,128)(2,1)} %bitcast.21), channel_id=1, replica_groups=mesh['term'=8,'topic'=4] {'topic'}, dimensions={0} | all-to-all | bytes 4194304 | tf_op jit(solution)/shard_map/all_to_all | solution.py:35
  62.0 3.9 %copy.9 = bf16[2048,4,128]{0,2,1:T(8,128)(2,1)} copy(bf16[2048,4,128]{2,0,1:T(8,128)(2,1)} %bitcast.22) | data formatting | bytes 4194304 | tf_op jit(solution)/shard_map/all_to_all | solution.py:35
  66.0 4.5 %fusion.7 = f32[512,512]{1,0:T(8,128)} fusion(bf16[2048,512]{0,1:T(8,128)(2,1)} %bitcast.23), kind=kOutput, calls=%fused_computation.14 | convolution fusion | flops 1073741824 | bytes 3145728 | tf_op jit(solution)/shard_map/dot_general | solution.py:12
  70.5 0.0 reduce-scatter.4.cloned.1.call-start
  70.6 0.8 convolution_convert_fusion
  71.4 1.3 copy-done.1
  72.7 1.3 convolution_bitcast_fusion
  74.1 0.0 all-reduce.2.cloned.1.call-start
  74.1 23.0 %reduce-scatter.6.cloned.1.call-done = f32[128,512]{1,0:T(8,128)} async-done(((f32[512,512]{1,0:T(8,128)}), f32[128,512]{1,0:T(8,128)}) %reduce-scatter.6.cloned.1.call-update) | async-done | bytes 262160 | tf_op jit(solution)/shard_map/reduce_scatter | solution.py:36
  97.2 0.0 reduce-scatter.8.cloned.1.call-start
  97.3 13.1 %all_gather.15 = f32[512,16]{0,1:T(8,128)S(1)} all-gather(f32[128,16]{0,1:T(8,128)S(1)} %copy-done.5), channel_id=1, replica_groups=mesh['term'=8,'topic'=4] {'topic'}, dimensions={0}, use_global_device_ids=true | all-gather | bytes 40960 | tf_op jit(solution)/shard_map/all_gather | solution.py:20
  110.4 22.4 %reduce-scatter.4.cloned.1.call-done = f32[128,16]{0,1:T(8,128)} async-done(((f32[128,128]{0,1:T(8,128)}), f32[128,16]{0,1:T(8,128)}) %reduce-scatter.4.cloned.1.call-update) | async-done | bytes 8208 | tf_op jit(solution)/shard_map/reduce_scatter | solution.py:34
  132.8 57.0 %all-reduce.2.cloned.1.call-done = f32[128,512]{1,0:T(8,128)} async-done(((f32[128,512]{1,0:T(8,128)}), f32[128,512]{1,0:T(8,128)}) %all-reduce.2.cloned.1.call-update) | async-done | bytes 262160 | tf_op jit(solution)/shard_map/psum | solution.py:39
  189.8 1.3 fusion.3
  191.0 13.2 %all_gather.16 = f32[512,16]{0,1:T(8,128)S(1)} all-gather(f32[128,16]{0,1:T(8,128)S(1)} %fusion.3), channel_id=1, replica_groups=mesh['term'=8,'topic'=4] {'topic'}, dimensions={0}, use_global_device_ids=true | all-gather | bytes 40960 | tf_op jit(solution)/shard_map/all_gather | solution.py:20
  204.2 1.3 fusion.2
  205.5 13.1 %all_gather.17 = f32[512,16]{0,1:T(8,128)S(1)} all-gather(f32[128,16]{0,1:T(8,128)S(1)} %fusion.2), channel_id=1, replica_groups=mesh['term'=8,'topic'=4] {'topic'}, dimensions={0}, use_global_device_ids=true | all-gather | bytes 40960 | tf_op jit(solution)/shard_map/all_gather | solution.py:20
  218.6 1.3 fusion.1
  219.9 8.6 %all_gather.19 = f32[128,128]{0,1:T(8,128)S(1)} all-gather(f32[128,16]{0,1:T(8,128)S(1)} %fusion.1), channel_id=1, replica_groups=mesh['term'=8,'topic'=4] {'term'}, dimensions={1}, use_global_device_ids=true | all-gather | bytes 73728 | tf_op jit(solution)/shard_map/all_gather | solution.py:52
  228.6 13.1 %all_gather.18 = f32[512,16]{0,1:T(8,128)S(1)} all-gather(f32[128,16]{0,1:T(8,128)S(1)} %fusion.1), channel_id=1, replica_groups=mesh['term'=8,'topic'=4] {'topic'}, dimensions={0}, use_global_device_ids=true | all-gather | bytes 40960 | tf_op jit(solution)/shard_map/all_gather | solution.py:45
  241.7 1.3 fusion.8
  243.0 7.4 %fusion = f32[8192,128]{1,0:T(8,128)} fusion(bf16[128,8192]{1,0:T(8,128)(2,1)} %copy-done.1, f32[128,128]{0,1:T(8,128)S(1)} %all_gather.19, f32[8192,128]{1,0:T(8,128)} %param.11), kind=kOutput, calls=%fused_computation.1 | convolution fusion | flops 1613758464 | bytes 10551296 | tf_op jit(solution)/shard_map/dot_general | solution.py:54
  250.4 26.5 %reduce-scatter.8.cloned.1.call-done = f32[128,64]{0,1:T(8,128)} async-done(((f32[128,512]{0,1:T(8,128)}), f32[128,64]{0,1:T(8,128)}) %reduce-scatter.8.cloned.1.call-update) | async-done | bytes 32784 | tf_op jit(solution)/shard_map/reduce_scatter | solution.py:50
  276.8 1.4 multiply_add_fusion
  (18 shorter events, 0.1 us)
Async XLA Ops:
  7.2 63.4 %copy-start = (bf16[8192,128]{1,0:T(8,128)(2,1)S(1)}, bf16[8192,128]{1,0:T(8,128)(2,1)}, u32[]{:S(2)}) copy-start(bf16[8192,128]{1,0:T(8,128)(2,1)} %param.7) | copy-start | bytes 6291460
  7.2 90.0 %reduce-scatter.6.cloned.1.call-start = ((), (), s32[]{:S(2)}) async-start(), calls=%async_computation.5 | async-start | bytes 1310720 | tf_op jit(solution)/shard_map/reduce_scatter | solution.py:36
  66.0 4.6 %copy-start.6 = (s32[1,128]{1,0:T(1,128)S(1)}, s32[1,128]{1,0:T(1,128)}, u32[]{:S(2)}) copy-start(s32[1,128]{1,0:T(1,128)} %param.8) | copy-start | bytes 1540
  70.5 62.3 %reduce-scatter.4.cloned.1.call-start = ((), (), s32[]{:S(2)}) async-start(), calls=%async_computation.4 | async-start | bytes 73728 | tf_op jit(solution)/shard_map/reduce_scatter | solution.py:34
  70.6 2.2 copy-start.2
  71.4 1.3 copy-start.1
  72.7 24.5 %copy-start.5 = (f32[128,16]{0,1:T(8,128)S(1)}, f32[128,16]{0,1:T(8,128)}, u32[]{:S(2)}) copy-start(f32[128,16]{0,1:T(8,128)} %param.9) | copy-start | bytes 24580
  74.1 115.7 %all-reduce.2.cloned.1.call-start = ((), (), s32[]{:S(2)}) async-start(), calls=%async_computation.6 | async-start | bytes 524288 | tf_op jit(solution)/shard_map/psum | solution.py:39
  97.2 179.6 %reduce-scatter.8.cloned.1.call-start = ((), (), s32[]{:S(2)}) async-start(), calls=%async_computation.7 | async-start | bytes 294912 | tf_op jit(solution)/shard_map/reduce_scatter | solution.py:50
  219.9 30.4 %copy-start.3 = (f32[128,16]{0,1:T(8,128)}, f32[128,16]{0,1:T(8,128)S(1)}, u32[]{:S(2)}) copy-start(f32[128,16]{0,1:T(8,128)S(1)} %fusion.1) | copy-start | bytes 24580
  243.0 33.8 %copy-start.4 = (f32[128,64]{0,1:T(8,128)S(1)}, f32[128,64]{0,1:T(8,128)}, u32[]{:S(2)}) copy-start(f32[128,64]{0,1:T(8,128)} %param.10) | copy-start | bytes 98308
Sparse Core Ops, SparseCore 0:
  70.6 26.5 reduce-scatter.5
  100.7 31.9 reduce-scatter.3
  135.8 53.8 all-reduce.1
  243.1 33.6 reduce-scatter.7
where the time goes:
time: 285 us
  waiting for transfers between devices  129 us (45%)
  blocking collectives  116 us (41%)
  matrix products  19.1 us (7%)
  between operations  13.9 us (5%)
  local copies, waits for them, and re-layouts  5.32 us (2%)
    psum x1, waiting for transfers between devices, per_device(): gram_rows = lax.psum(gram_part, 'term')  57 us
    all_to_all x1, blocking collectives, per_device(): lax.all_to_all(factor, 'topic', split_axis=0, concat_axis=1, tiled=True)  54.8 us
    all_gather x3, blocking collectives, apply_gram(): lax.all_gather(current, 'topic', axis=0, tiled=True)  39.5 us
    reduce_scatter x1, waiting for transfers between devices, per_device(): lax.psum_scatter(outer, 'term', scatter_dimension=1, tiled=True)  26.5 us
    reduce_scatter x1, waiting for transfers between devices, per_device(): lax.psum_scatter(contract_rows(row_block, row_block), 'topic', scatter_di...  23 us
    reduce_scatter x1, waiting for transfers between devices, per_device(): lax.psum_scatter(partial_data, 'term', scatter_dimension=1, tiled=True)  22.4 us
    all_gather x1, blocking collectives, per_device(): lax.all_gather(current, 'topic', axis=0, tiled=True)  13.1 us
    all_gather x1, blocking collectives, per_device(): code_row = lax.all_gather(current, 'term', axis=1, tiled=True)  8.61 us
  transfers between devices with their start and end apart: 4, of which 4 were waited for; matrix products, arithmetic and copies ran while one was open for 3% of the time, Pallas kernels for 0%

commit v1 on v0

--- a/solution.py
+++ b/solution.py
@@ -36,7 +36,26 @@
     gram_part = lax.psum_scatter(
         contract_rows(row_block, row_block), "topic", scatter_dimension=0, tiled=True
     )
-    gram_rows = lax.psum(gram_part, "term")
+
+    def edit_series_all(inputs):
+        chip_axis = "term"
+        full_n = lax.psum(1, axis_name=chip_axis)
+
+        def see_the_copies(carry, item_now):
+            if item_now >= full_n:
+                return carry
+            then = lax.ppermute(
+                carry,
+                axis_name=chip_axis,
+                perm=tuple(((dev, dev ^ item_now) for dev in range(full_n))),
+            )
+            tmp = see_the_copies(carry + then, 2 * item_now)
+            return tmp
+
+        v1 = see_the_copies(inputs, 1)
+        return v1
+
+    gram_rows = edit_series_all(gram_part)
     current = codes
     for update in range(ITERS):
         current = current * data_share / (apply_gram(gram_rows, current) + EPSILON)

time: 285 us -> 240 us (0.84)
  waiting for transfers between devices: 129 us -> 78.9 us
  starting transfers between devices: 0.16 us -> 3.18 us
    psum x1 -> x0, waiting for transfers between devices: 57 us -> none  [per_device(): gram_rows = lax.psum(gram_part, 'term')]
    ppermute x0 -> x3, waiting for transfers between devices: none -> 7.79 us  [see_the_copies(): lax.ppermute(carry, axis_name=chip_axis, perm=tuple(((dev, dev ^ item_now...]
    reduce_scatter x1, waiting for transfers between devices: 22.4 us -> 18 us  [per_device(): lax.psum_scatter(partial_data, 'term', scatter_dimension=1, tiled=True)]
    reduce_scatter x1, waiting for transfers between devices: 23 us -> 26.6 us  [per_device(): lax.psum_scatter(contract_rows(row_block, row_block), 'topic', scatter_di...]
    ppermute x0 -> x3, starting transfers between devices: none -> 3.06 us  [see_the_copies(): lax.ppermute(carry, axis_name=chip_axis, perm=tuple(((dev, dev ^ item_now...]
  transfers between devices with their start and end apart: 4 -> 6, of which waited for: 4 -> 5; matrix products, arithmetic and copies ran while one was open for 3% -> 4% of each run, Pallas kernels for 0% -> 0%
where the time goes in v1:
time: 240 us; the launch traced here: 239 us
  blocking collectives  117 us (49%)
  waiting for transfers between devices  78.9 us (33%)
  matrix products  18.4 us (8%)
  between operations  15.6 us (6%)
  local copies, waits for them, and re-layouts  3.98 us (2%)
  starting transfers between devices  3.18 us (1%)
  other arithmetic  2.44 us (1%)
    all_to_all x1, blocking collectives, per_device(): lax.all_to_all(factor, 'topic', split_axis=0, concat_axis=1, tiled=True)  54.8 us
    all_gather x3, blocking collectives, apply_gram(): lax.all_gather(current, 'topic', axis=0, tiled=True)  39.5 us
    reduce_scatter x1, waiting for transfers between devices, per_device(): lax.psum_scatter(contract_rows(row_block, row_block), 'topic', scatter_di...  26.6 us
    reduce_scatter x1, waiting for transfers between devices, per_device(): lax.psum_scatter(outer, 'term', scatter_dimension=1, tiled=True)  26.4 us
    reduce_scatter x1, waiting for transfers between devices, per_device(): lax.psum_scatter(partial_data, 'term', scatter_dimension=1, tiled=True)  18 us
    all_gather x1, blocking collectives, per_device(): lax.all_gather(current, 'topic', axis=0, tiled=True)  13.1 us
    all_gather x1, blocking collectives, per_device(): code_row = lax.all_gather(current, 'term', axis=1, tiled=True)  9.2 us
    ppermute x3, waiting for transfers between devices, see_the_copies(): lax.ppermute(carry, axis_name=chip_axis, perm=tuple(((dev, dev ^ item_now...  7.79 us
  transfers between devices with their start and end apart: 6, of which 5 were waited for; matrix products, arithmetic and copies ran while one was open for 4% of the time, Pallas kernels for 0%

profile of v1, /device:TPU:0, one launch (start us, length us, event | category | flops | bytes accessed | tf_op | source)
XLA Modules:
  0.0 239.0 jit_solution(4860731499453757168)
XLA Ops:
  8.1 54.8 %all_to_all.19 = bf16[4,2048,128]{2,1,0:T(8,128)(2,1)} all-to-all(bf16[4,2048,128]{2,1,0:T(8,128)(2,1)} %bitcast.21), channel_id=1, replica_groups=mesh['term'=8,'topic'=4] {'topic'}, dimensions={0} | all-to-all | bytes 4194304 | tf_op jit(solution)/shard_map/all_to_all | solution.py:35
  62.8 3.9 %copy.9 = bf16[2048,4,128]{0,2,1:T(8,128)(2,1)} copy(bf16[2048,4,128]{2,0,1:T(8,128)(2,1)} %bitcast.22) | data formatting | bytes 4194304 | tf_op jit(solution)/shard_map/all_to_all | solution.py:35
  66.8 4.5 %fusion.7 = f32[512,512]{1,0:T(8,128)} fusion(bf16[2048,512]{0,1:T(8,128)(2,1)} %bitcast.23), kind=kOutput, calls=%fused_computation.14 | convolution fusion | flops 1073741824 | bytes 3145728 | tf_op jit(solution)/shard_map/dot_general | solution.py:12
  71.4 26.6 %reduce-scatter.6.cloned.1.call-done = f32[128,512]{1,0:T(8,128)} async-done(((f32[512,512]{1,0:T(8,128)}), f32[128,512]{1,0:T(8,128)}) %reduce-scatter.6.cloned.1.call-update) | async-done | bytes 262160 | tf_op jit(solution)/shard_map/reduce_scatter | solution.py:36
  98.0 1.7 collective-permute-done
  99.7 1.0 add.30
  100.7 1.5 collective-permute-start.1
  102.3 0.8 convolution_convert_fusion
  103.1 6.0 %collective-permute-done.1 = f32[128,512]{1,0:T(8,128)S(1)} collective-permute-done((f32[128,512]{1,0:T(8,128)S(1)}, f32[128,512]{1,0:T(8,128)S(1)}, u32[]{:S(2)}, u32[]{:S(2)}) %collective-permute-start.1) | collective-permute-done | bytes 262176 | tf_op jit(solution)/shard_map/ppermute | solution.py:47
  109.2 1.5 collective-permute-start.2
  110.7 1.3 convolution_bitcast_fusion
  112.1 13.1 %all_gather.15 = f32[512,16]{0,1:T(8,128)S(1)} all-gather(f32[128,16]{0,1:T(8,128)S(1)} %copy-done.5), channel_id=1, replica_groups=mesh['term'=8,'topic'=4] {'topic'}, dimensions={0}, use_global_device_ids=true | all-gather | bytes 40960 | tf_op jit(solution)/shard_map/all_gather | solution.py:20
  125.3 18.0 %reduce-scatter.4.cloned.1.call-done = f32[128,16]{0,1:T(8,128)} async-done(((f32[128,128]{0,1:T(8,128)}), f32[128,16]{0,1:T(8,128)}) %reduce-scatter.4.cloned.1.call-update) | async-done | bytes 8208 | tf_op jit(solution)/shard_map/reduce_scatter | solution.py:34
  143.3 1.0 fusion.3
  144.3 13.2 %all_gather.16 = f32[512,16]{0,1:T(8,128)S(1)} all-gather(f32[128,16]{0,1:T(8,128)S(1)} %fusion.3), channel_id=1, replica_groups=mesh['term'=8,'topic'=4] {'topic'}, dimensions={0}, use_global_device_ids=true | all-gather | bytes 40960 | tf_op jit(solution)/shard_map/all_gather | solution.py:20
  157.5 1.0 fusion.2
  158.6 13.1 %all_gather.17 = f32[512,16]{0,1:T(8,128)S(1)} all-gather(f32[128,16]{0,1:T(8,128)S(1)} %fusion.2), channel_id=1, replica_groups=mesh['term'=8,'topic'=4] {'topic'}, dimensions={0}, use_global_device_ids=true | all-gather | bytes 40960 | tf_op jit(solution)/shard_map/all_gather | solution.py:20
  171.7 1.0 fusion.1
  172.7 9.2 %all_gather.19 = f32[128,128]{0,1:T(8,128)S(1)} all-gather(f32[128,16]{0,1:T(8,128)S(1)} %fusion.1), channel_id=1, replica_groups=mesh['term'=8,'topic'=4] {'term'}, dimensions={1}, use_global_device_ids=true | all-gather | bytes 73728 | tf_op jit(solution)/shard_map/all_gather | solution.py:71
  181.9 13.1 %all_gather.18 = f32[512,16]{0,1:T(8,128)S(1)} all-gather(f32[128,16]{0,1:T(8,128)S(1)} %fusion.1), channel_id=1, replica_groups=mesh['term'=8,'topic'=4] {'topic'}, dimensions={0}, use_global_device_ids=true | all-gather | bytes 40960 | tf_op jit(solution)/shard_map/all_gather | solution.py:64
  195.1 1.3 fusion.8
  196.4 7.4 %fusion = f32[8192,128]{1,0:T(8,128)} fusion(bf16[128,8192]{1,0:T(8,128)(2,1)} %copy-done.1, f32[128,128]{0,1:T(8,128)S(1)} %all_gather.19, f32[8192,128]{1,0:T(8,128)} %param.11), kind=kOutput, calls=%fused_computation.1 | convolution fusion | flops 1613758464 | bytes 10551296 | tf_op jit(solution)/shard_map/dot_general | solution.py:73
  203.8 26.4 %reduce-scatter.8.cloned.1.call-done = f32[128,64]{0,1:T(8,128)} async-done(((f32[128,512]{0,1:T(8,128)}), f32[128,64]{0,1:T(8,128)}) %reduce-scatter.8.cloned.1.call-update) | async-done | bytes 32784 | tf_op jit(solution)/shard_map/reduce_scatter | solution.py:69
  230.2 1.4 multiply_add_fusion
  (24 shorter events, 0.3 us)
Async XLA Ops:
  8.0 94.3 %copy-start = (bf16[8192,128]{1,0:T(8,128)(2,1)S(1)}, bf16[8192,128]{1,0:T(8,128)(2,1)}, u32[]{:S(2)}) copy-start(bf16[8192,128]{1,0:T(8,128)(2,1)} %param.7) | copy-start | bytes 6291460
  8.0 90.0 %reduce-scatter.6.cloned.1.call-start = ((), (), s32[]{:S(2)}) async-start(), calls=%async_computation.5 | async-start | bytes 1310720 | tf_op jit(solution)/shard_map/reduce_scatter | solution.py:36
  66.8 35.5 %copy-start.6 = (s32[1,128]{1,0:T(1,128)S(1)}, s32[1,128]{1,0:T(1,128)}, u32[]{:S(2)}) copy-start(s32[1,128]{1,0:T(1,128)} %param.8) | copy-start | bytes 1540
  71.3 72.0 %reduce-scatter.4.cloned.1.call-start = ((), (), s32[]{:S(2)}) async-start(), calls=%async_computation.4 | async-start | bytes 73728 | tf_op jit(solution)/shard_map/reduce_scatter | solution.py:34
  98.0 1.7 collective-permute-start
  100.7 8.4 %collective-permute-start.1 = (f32[128,512]{1,0:T(8,128)S(1)}, f32[128,512]{1,0:T(8,128)S(1)}, u32[]{:S(2)}, u32[]{:S(2)}) collective-permute-start(f32[128,512]{1,0:T(8,128)S(1)} %add.30), channel_id=1, source_target_pairs={{0,8},{4,12},{8,0},{12,4},{16,24},{20,28},{24,16},{28,20},{1,9},{5... | collective-permute-start | bytes 786440 | tf_op jit(solution)/shard_map/ppermute | solution.py:47
  102.3 8.5 %copy-start.2 = (bf16[8192,128]{1,0:T(8,128)(2,1)S(1)}, bf16[8192,128]{1,0:T(8,128)(2,1)}, u32[]{:S(2)}) copy-start(bf16[8192,128]{1,0:T(8,128)(2,1)} %param.6) | copy-start | bytes 6291460
  103.1 7.6 %copy-start.1 = (bf16[128,8192]{1,0:T(8,128)(2,1)}, bf16[128,8192]{1,0:T(8,128)(2,1)S(1)}, u32[]{:S(2)}) copy-start(bf16[128,8192]{1,0:T(8,128)(2,1)S(1)} %convolution_convert_fusion) | copy-start | bytes 6291460
  109.2 3.0 %copy-start.5 = (f32[128,16]{0,1:T(8,128)S(1)}, f32[128,16]{0,1:T(8,128)}, u32[]{:S(2)}) copy-start(f32[128,16]{0,1:T(8,128)} %param.9) | copy-start | bytes 24580
  109.2 16.1 %collective-permute-start.2 = (f32[128,512]{1,0:T(8,128)S(1)}, f32[128,512]{1,0:T(8,128)S(1)}, u32[]{:S(2)}, u32[]{:S(2)}) collective-permute-start(f32[128,512]{1,0:T(8,128)S(1)} %add.31), channel_id=1, source_target_pairs={{0,16},{4,20},{8,24},{12,28},{16,0},{20,4},{24,8},{28,12},{1,17},{... | collective-permute-start | bytes 786440 | tf_op jit(solution)/shard_map/ppermute | solution.py:47
  112.1 118.1 %reduce-scatter.8.cloned.1.call-start = ((), (), s32[]{:S(2)}) async-start(), calls=%async_computation.6 | async-start | bytes 294912 | tf_op jit(solution)/shard_map/reduce_scatter | solution.py:69
  172.7 31.0 %copy-start.3 = (f32[128,16]{0,1:T(8,128)}, f32[128,16]{0,1:T(8,128)S(1)}, u32[]{:S(2)}) copy-start(f32[128,16]{0,1:T(8,128)S(1)} %fusion.1) | copy-start | bytes 24580
  196.4 33.8 %copy-start.4 = (f32[128,64]{0,1:T(8,128)S(1)}, f32[128,64]{0,1:T(8,128)}, u32[]{:S(2)}) copy-start(f32[128,64]{0,1:T(8,128)} %param.10) | copy-start | bytes 98308
Sparse Core Ops, SparseCore 0:
  71.4 26.5 reduce-scatter.5
Sparse Core Ops, SparseCore 1:
  112.2 31.1 reduce-scatter.3
  196.5 33.7 reduce-scatter.7
